TPU v7x, 128 devices: a whole 4x4x4 slice. The times are simulated.
128 devices in a mesh: seq: 16 (over x_lo, y, core), heads: 8 (over z, x_hi).
Axes of the slice: x: 4 (x_hi: 2, x_lo: 2; x = x_hi * 2 + x_lo), y: 4, z: 4, core: 2. Of those that a mesh axis runs over, the one named last changes fastest.
Arguments:
- hidden_in: bfloat16 [4096, 8192], P('seq', 'heads'), may hold values from -6 to 6
- queries: bfloat16 [4096, 8192], P('seq', 'heads'), as said below
- image_kv: bfloat16 [16, 2, 6528, 1024], P('seq', None, None, 'heads'), as said below
- out_weight: bfloat16 [8192, 8192], P('seq', 'heads'), may hold values from -0.0625 to 0.0625
- gate: float32 [1], replicated, may hold values from 0.4 to 1.2
- tile_counts: int32 [16], replicated, may hold values from 1 to 4, as said below
- owners: int32 [256], replicated, may hold values from 0 to 15, as said below
- starts: int32 [256], replicated, may hold values from 0 to 3, as said below
- norm_gain: float32 [8192], P('heads'), may hold values from 0.1 to 1.9
- norm_grad: bfloat16 [4096, 8192], P('seq', 'heads'), may hold values from -6 to 6
- stream_grad: bfloat16 [4096, 8192], P('seq', 'heads'), may hold values from -6 to 6
Outputs:
- hidden_out: bfloat16 [4096, 8192], P('seq', 'heads')
- stream_in_grad: float32 [4096, 8192], P('seq', 'heads')
Inputs may be any that keep to these rules, and one draw needn't show every extreme that they name: `tile_counts`: tiles of each image; some image has 4 tiles in every draw. `owners`: the image (named by the seq index that owns it) that a block of 16 text rows attends to; of the 16 blocks of one seq index at most 2 name the same image, and in every draw some image is named by exactly 2 blocks of every seq index. `starts`: the first tile a block sees, below the tile count of the block's image; in every draw some block starts at tile 0 and some at tile 4 - 1. `image_kv`: keys and values are real-valued. real-valued queries.
All inputs are finite; a program needn't handle non-finite values.
Results may differ from a plain program's by a relative error of at most 0.007.
Values may be sent and summed in bfloat16 or wider, within the bound.
No kernel may reach another device: no remote copies, remote signals or barrier semaphores. Data moves between devices by JAX's collectives and lax.ppermute only.
A program may use at most 128 MiB of HBM per device.

v0:
```python
import math
import jax
import jax.numpy as jnp
from jax import lax
from jax.sharding import PartitionSpec as P

D = 8192
HEAD_DIM = 128
TILE_TOK = 1601
BLOCKS_DEV = 16
CAP = 2
BLK = 16
EPS = 1e-05


def head_scores(query_head, key_block, scale):
    return (
        lax.dot_general(
            query_head, key_block, (((1,), (1,)), ((), ())), preferred_element_type=jnp.float32
        )
        * scale
    )


def local(
    hidden_in,
    queries,
    image_kv,
    out_weight,
    gate,
    tile_counts,
    owners,
    starts,
    norm_gain,
    norm_grad,
    stream_grad,
):
    seq_count = lax.axis_size("seq")
    here = lax.axis_index("seq")
    tok_rows, q_width = queries.shape
    q_heads = q_width // HEAD_DIM
    slot_count = seq_count * CAP
    scale = 1.0 / math.sqrt(HEAD_DIM)
    owner_table = owners.reshape(seq_count, BLOCKS_DEV)
    start_table = starts.reshape(seq_count, BLOCKS_DEV)
    my_owner = lax.dynamic_index_in_dim(owner_table, here, 0, keepdims=False)
    block_ids = jnp.arange(BLOCKS_DEV)
    same = my_owner[:, None] == my_owner[None, :]
    earlier = block_ids[None, :] < block_ids[:, None]
    my_rank = jnp.sum(jnp.logical_and(same, earlier).astype(jnp.int32), axis=1)
    my_slot = my_owner * CAP + my_rank
    placing = (my_slot[:, None] == jnp.arange(slot_count)[None, :]).astype(jnp.bfloat16)
    q_blocks = queries.reshape(BLOCKS_DEV, BLK, q_width)
    outgoing = jnp.einsum(
        "bs,brc->src", placing, q_blocks, preferred_element_type=jnp.float32
    ).astype(jnp.bfloat16)
    outgoing = outgoing.reshape(seq_count, CAP, BLK, q_width)
    arriving = owner_table == here
    arrive_rank = jnp.cumsum(arriving.astype(jnp.int32), axis=1) - 1
    slot_hit = jnp.logical_and(
        arriving[:, :, None], arrive_rank[:, :, None] == jnp.arange(CAP)[None, None, :]
    )
    slot_start = jnp.sum(jnp.where(slot_hit, start_table[:, :, None], 0), axis=1)
    tile_here = lax.dynamic_index_in_dim(tile_counts, here, 0, keepdims=False)
    key_end = tile_here * TILE_TOK
    keys_here = image_kv[0, 0]
    values_here = image_kv[0, 1]
    received = lax.all_to_all(outgoing, "seq", split_axis=0, concat_axis=0, tiled=True)
    flat = received.reshape(-1, q_width)
    row_first = jnp.broadcast_to(slot_start[:, :, None], received.shape[:3]).reshape(-1) * TILE_TOK

    def one_head(head):
        query_head = lax.dynamic_slice_in_dim(flat, head * HEAD_DIM, HEAD_DIM, 1)
        spot = jnp.arange(keys_here.shape[0])
        seen = jnp.logical_and(spot[None, :] >= row_first[:, None], spot[None, :] < key_end)
        scores = jnp.where(seen, head_scores(query_head, keys_here, scale), -jnp.inf)
        highest = jnp.max(scores, axis=1, keepdims=True)
        probs = jnp.exp(scores - highest)
        total = jnp.sum(probs, axis=1, keepdims=True)
        mixed = jnp.dot(probs.astype(jnp.bfloat16), values_here, preferred_element_type=jnp.float32)
        return (mixed / total).astype(jnp.bfloat16)

    heads_out = lax.map(one_head, jnp.arange(q_heads))
    merged = jnp.moveaxis(heads_out, 0, 1).reshape(received.shape)
    returned = lax.all_to_all(merged, "seq", split_axis=0, concat_axis=0, tiled=True)
    context = jnp.einsum(
        "bs,src->brc",
        placing,
        returned.reshape(slot_count, BLK, q_width),
        preferred_element_type=jnp.float32,
    )
    context = context.astype(jnp.bfloat16).reshape(tok_rows, q_width)
    full_context = lax.all_gather(context, "heads", axis=1, tiled=True)
    branch = jnp.dot(
        full_context,
        lax.all_gather(out_weight, "seq", axis=0, tiled=True),
        preferred_element_type=jnp.float32,
    )
    hidden_out = (hidden_in.astype(jnp.float32) + jnp.tanh(gate[0]) * branch).astype(jnp.bfloat16)
    hidden = hidden_out.astype(jnp.float32)
    scaled = norm_gain[None, :] * norm_grad.astype(jnp.float32)
    squares, product = lax.psum(
        (jnp.sum(hidden * hidden, axis=1), jnp.sum(hidden * scaled, axis=1)), "heads"
    )
    inverse = lax.rsqrt(squares / D + EPS)[:, None]
    project = (product / D)[:, None]
    stream_in_grad = (
        stream_grad.astype(jnp.float32) + inverse * scaled - inverse**3 * project * hidden
    )
    return (hidden_out, stream_in_grad)


def solution(mesh):
    placed = (
        P("seq", "heads"),
        P("seq", "heads"),
        P("seq", None, None, "heads"),
        P("seq", "heads"),
        P(),
        P(),
        P(),
        P(),
        P("heads"),
        P("seq", "heads"),
        P("seq", "heads"),
    )
    return jax.shard_map(
        local,
        mesh=mesh,
        in_specs=placed,
        out_specs=(P("seq", "heads"), P("seq", "heads")),
        check_vma=False,
    )
```

profile of v0, /device:TPU:0, one launch (start us, length us, event | category | flops | bytes accessed | tf_op | source)
XLA Modules:
  0.0 361.5 jit_solution(7062695272086445816)
XLA Ops:
  7.2 0.8 reshape.76
  9.3 2.0 copy.36
  11.2 5.7 %all-to-all-start = ((bf16[16,2,16,1024]{3,1,2,0:T(2,128)(2,1)}), bf16[16,2,16,1024]{3,1,2,0:T(2,128)(2,1)}, u32[]{:S(2)}, u32[]{:S(2)}) async-start(bf16[16,2,16,1024]{3,1,2,0:T(2,128)(2,1)} %copy.36), calls=%async_computation | async-start | bytes 2097152 | tf_op jit(solution)/shard_map/all_to_all | solution.py:68
  18.6 3.4 slice_bitcast_fusion
  21.9 11.6 %all-to-all-done = bf16[16,2,16,1024]{3,1,2,0:T(2,128)(2,1)} async-done(((bf16[16,2,16,1024]{3,1,2,0:T(2,128)(2,1)}), bf16[16,2,16,1024]{3,1,2,0:T(2,128)(2,1)}, u32[]{:S(2)}, u32[]{:S(2)}) %all-to-all-start) | async-done | bytes 1048608 | tf_op jit(solution)/shard_map/all_to_all | solution.py:68
  33.5 2.5 copy.37
  36.0 95.0 %while.11 = (s32[]{:T(128)}, bf16[8,512,128]{2,1,0:T(8,128)(2,1)}, s32[]{:T(128)}, s32[8]{0:T(128)S(1)}, bf16[512,1024]{1,0:T(8,128)(2,1)}, /*index=5*/bf16[6528...) while((s32[]{:T(128)}, bf16[8,512,128]{2,1,0:T(8,128)(2,1)}, ...), condition=%wide.region_6.7_spmd.clone, body=%wide.region_3.6_spmd.clone.sunk | while | flops 1741493632 | bytes 43744824 | solution.py:83
  36.0 0.6 dynamic_slice.29
  37.5 5.6 %fusion.52 = (f32[512]{0:T(512)S(1)}, f32[512,6528]{1,0:T(8,128)S(1)}) fusion(bf16[6528,128]{1,0:T(8,128)(2,1)} %get-tuple-element.183, bf16[512,1024]{1,0:T(8,128)(2,1)} %get-tuple-element.182, s32[]{:T(128)S(6)} %select_n.24, pred[6528]{0:T(1024)(128)(4,1)S(1)} %iota_compare_fusion.6, s32[512]{0:T(512)S(1)} %mul.129), kind=kOutput, calls=%fused_computation.51.clone.1 | convolution fusion | flops 872349184 | bytes 15182212 | tf_op jit(solution)/shard_map/while/body/eval_jaxpr/dot_general | solution.py:18
  43.1 2.1 fusion.53
  45.2 2.7 fusion.54
  47.9 0.6 dynamic_slice.29
  49.3 5.6 %fusion.52 = (f32[512]{0:T(512)S(1)}, f32[512,6528]{1,0:T(8,128)S(1)}) fusion(bf16[6528,128]{1,0:T(8,128)(2,1)} %get-tuple-element.183, bf16[512,1024]{1,0:T(8,128)(2,1)} %get-tuple-element.182, s32[]{:T(128)S(6)} %select_n.24, pred[6528]{0:T(1024)(128)(4,1)S(1)} %iota_compare_fusion.6, s32[512]{0:T(512)S(1)} %mul.129), kind=kOutput, calls=%fused_computation.51.clone.1 | convolution fusion | flops 872349184 | bytes 15182212 | tf_op jit(solution)/shard_map/while/body/eval_jaxpr/dot_general | solution.py:18
  54.9 2.1 fusion.53
  57.0 2.7 fusion.54
  59.7 0.6 dynamic_slice.29
  61.2 5.6 %fusion.52 = (f32[512]{0:T(512)S(1)}, f32[512,6528]{1,0:T(8,128)S(1)}) fusion(bf16[6528,128]{1,0:T(8,128)(2,1)} %get-tuple-element.183, bf16[512,1024]{1,0:T(8,128)(2,1)} %get-tuple-element.182, s32[]{:T(128)S(6)} %select_n.24, pred[6528]{0:T(1024)(128)(4,1)S(1)} %iota_compare_fusion.6, s32[512]{0:T(512)S(1)} %mul.129), kind=kOutput, calls=%fused_computation.51.clone.1 | convolution fusion | flops 872349184 | bytes 15182212 | tf_op jit(solution)/shard_map/while/body/eval_jaxpr/dot_general | solution.py:18
  66.8 2.1 fusion.53
  68.9 2.7 fusion.54
  71.6 0.6 dynamic_slice.29
  73.1 5.6 %fusion.52 = (f32[512]{0:T(512)S(1)}, f32[512,6528]{1,0:T(8,128)S(1)}) fusion(bf16[6528,128]{1,0:T(8,128)(2,1)} %get-tuple-element.183, bf16[512,1024]{1,0:T(8,128)(2,1)} %get-tuple-element.182, s32[]{:T(128)S(6)} %select_n.24, pred[6528]{0:T(1024)(128)(4,1)S(1)} %iota_compare_fusion.6, s32[512]{0:T(512)S(1)} %mul.129), kind=kOutput, calls=%fused_computation.51.clone.1 | convolution fusion | flops 872349184 | bytes 15182212 | tf_op jit(solution)/shard_map/while/body/eval_jaxpr/dot_general | solution.py:18
  78.7 2.1 fusion.53
  80.8 2.7 fusion.54
  83.5 0.6 dynamic_slice.29
  84.9 5.6 %fusion.52 = (f32[512]{0:T(512)S(1)}, f32[512,6528]{1,0:T(8,128)S(1)}) fusion(bf16[6528,128]{1,0:T(8,128)(2,1)} %get-tuple-element.183, bf16[512,1024]{1,0:T(8,128)(2,1)} %get-tuple-element.182, s32[]{:T(128)S(6)} %select_n.24, pred[6528]{0:T(1024)(128)(4,1)S(1)} %iota_compare_fusion.6, s32[512]{0:T(512)S(1)} %mul.129), kind=kOutput, calls=%fused_computation.51.clone.1 | convolution fusion | flops 872349184 | bytes 15182212 | tf_op jit(solution)/shard_map/while/body/eval_jaxpr/dot_general | solution.py:18
  90.6 2.1 fusion.53
  92.7 2.7 fusion.54
  95.3 0.6 dynamic_slice.29
  96.8 5.6 %fusion.52 = (f32[512]{0:T(512)S(1)}, f32[512,6528]{1,0:T(8,128)S(1)}) fusion(bf16[6528,128]{1,0:T(8,128)(2,1)} %get-tuple-element.183, bf16[512,1024]{1,0:T(8,128)(2,1)} %get-tuple-element.182, s32[]{:T(128)S(6)} %select_n.24, pred[6528]{0:T(1024)(128)(4,1)S(1)} %iota_compare_fusion.6, s32[512]{0:T(512)S(1)} %mul.129), kind=kOutput, calls=%fused_computation.51.clone.1 | convolution fusion | flops 872349184 | bytes 15182212 | tf_op jit(solution)/shard_map/while/body/eval_jaxpr/dot_general | solution.py:18
  102.4 2.1 fusion.53
  104.5 2.7 fusion.54
  107.2 0.6 dynamic_slice.29
  108.7 5.6 %fusion.52 = (f32[512]{0:T(512)S(1)}, f32[512,6528]{1,0:T(8,128)S(1)}) fusion(bf16[6528,128]{1,0:T(8,128)(2,1)} %get-tuple-element.183, bf16[512,1024]{1,0:T(8,128)(2,1)} %get-tuple-element.182, s32[]{:T(128)S(6)} %select_n.24, pred[6528]{0:T(1024)(128)(4,1)S(1)} %iota_compare_fusion.6, s32[512]{0:T(512)S(1)} %mul.129), kind=kOutput, calls=%fused_computation.51.clone.1 | convolution fusion | flops 872349184 | bytes 15182212 | tf_op jit(solution)/shard_map/while/body/eval_jaxpr/dot_general | solution.py:18
  114.3 2.1 fusion.53
  116.4 2.7 fusion.54
  119.1 0.6 dynamic_slice.29
  120.6 5.6 %fusion.52 = (f32[512]{0:T(512)S(1)}, f32[512,6528]{1,0:T(8,128)S(1)}) fusion(bf16[6528,128]{1,0:T(8,128)(2,1)} %get-tuple-element.183, bf16[512,1024]{1,0:T(8,128)(2,1)} %get-tuple-element.182, s32[]{:T(128)S(6)} %select_n.24, pred[6528]{0:T(1024)(128)(4,1)S(1)} %iota_compare_fusion.6, s32[512]{0:T(512)S(1)} %mul.129), kind=kOutput, calls=%fused_computation.51.clone.1 | convolution fusion | flops 872349184 | bytes 15182212 | tf_op jit(solution)/shard_map/while/body/eval_jaxpr/dot_general | solution.py:18
  126.2 2.1 fusion.53
  128.3 2.7 fusion.54
  131.0 2.0 copy.39
  133.4 19.1 %all_to_all.10 = bf16[16,2,16,1024]{3,2,1,0:T(8,128)(2,1)S(1)} all-to-all(bf16[16,2,16,1024]{3,2,1,0:T(8,128)(2,1)S(1)} %reshape.80), channel_id=1, replica_groups=mesh['seq'=16,'heads'=8] {'seq'}, dimensions={0} | all-to-all | bytes 2097152 | tf_op jit(solution)/shard_map/all_to_all | solution.py:85
  152.5 1.2 convolution_convert_fusion.1
  153.7 1.1 copy.41
  156.3 69.8 %all-gather.3.cloned.1.call-done = bf16[256,8192]{1,0:T(8,128)(2,1)} async-done(((bf16[256,1024]{1,0:T(8,128)(2,1)}), bf16[256,8192]{1,0:T(8,128)(2,1)}) %all-gather.3.cloned.1.call-update) | async-done | bytes 4194320 | tf_op jit(solution)/shard_map/all_gather | solution.py:93
  226.0 91.0 %all-gather.5.cloned.1.call-done = bf16[8192,1024]{1,0:T(8,128)(2,1)} async-done(((bf16[512,1024]{1,0:T(8,128)(2,1)}), bf16[8192,1024]{1,0:T(8,128)(2,1)}) %all-gather.5.cloned.1.call-update) | async-done | bytes 16777232 | tf_op jit(solution)/shard_map/all_gather | solution.py:96
  317.1 11.8 %fusion.24 = (f32[256]{0:T(256)S(1)}, f32[256]{0:T(256)S(1)}, bf16[256,1024]{1,0:T(8,128)(2,1)S(1)}) fusion(bf16[256,1024]{1,0:T(8,128)(2,1)S(1)} %copy-done.1, f32[1024]{0:T(1024)S(1)} %copy-done.4, bf16[256,8192]{1,0:T(8,128)(2,1)} %all-gather.3.cloned.1.call-done, bf16[8192,1024]{1,0:T(8,128)(2,1)} %all-gather.5.cloned.1.call-done, f32[]{:T(128)} %bitcast, ...), kind=kOutput, calls=%fused_computation.26 | convolution fusion | flops 4297850880 | bytes 22550532 | tf_op jit(solution)/shard_map/dot_general | solution.py:94
  328.9 24.4 %all-reduce = (f32[256]{0:T(256)S(1)}, f32[256]{0:T(256)S(1)}) all-reduce(f32[256]{0:T(256)S(1)} %get-tuple-element.73, f32[256]{0:T(256)S(1)} %get-tuple-element.72), channel_id=1, replica_groups=mesh['seq'=16,'heads'=8] {'heads'}, use_global_device_ids=true, to_apply=%region_10.11 | all-reduce | flops 512 | bytes 4096 | tf_op jit(solution)/shard_map/psum | solution.py:102
  353.4 1.3 fusion.26
  (59 shorter events, 5.0 us)
Async XLA Ops:
  7.2 1.1 copy-start
  7.2 10.0 %copy-start.5 = (s32[256]{0:T(256)S(1)}, s32[256]{0:T(256)}, u32[]{:S(2)}) copy-start(s32[256]{0:T(256)} %param.20) | copy-start | bytes 3076
  7.2 10.3 %copy-start.6 = (s32[16]{0:T(128)S(1)}, s32[16]{0:T(128)}, u32[]{:S(2)}) copy-start(s32[16]{0:T(128)} %param.18) | copy-start | bytes 196
  11.2 22.3 %all-to-all-start = ((bf16[16,2,16,1024]{3,1,2,0:T(2,128)(2,1)}), bf16[16,2,16,1024]{3,1,2,0:T(2,128)(2,1)}, u32[]{:S(2)}, u32[]{:S(2)}) async-start(bf16[16,2,16,1024]{3,1,2,0:T(2,128)(2,1)} %copy.36), calls=%async_computation | async-start | bytes 2097152 | tf_op jit(solution)/shard_map/all_to_all | solution.py:68
  16.9 209.1 %all-gather.3.cloned.1.call-start = ((), (), s32[]{:S(2)}) async-start(), calls=%async_computation.2 | async-start | bytes 4718592 | tf_op jit(solution)/shard_map/all_gather | solution.py:93
  131.0 186.1 %copy-start.1 = (bf16[256,1024]{1,0:T(8,128)(2,1)S(1)}, bf16[256,1024]{1,0:T(8,128)(2,1)}, u32[]{:S(2)}) copy-start(bf16[256,1024]{1,0:T(8,128)(2,1)} %param.22) | copy-start | bytes 1572868
  131.0 186.1 %copy-start.4 = (f32[1024]{0:T(1024)S(1)}, f32[1024]{0:T(1024)}, u32[]{:S(2)}) copy-start(f32[1024]{0:T(1024)} %param.21) | copy-start | bytes 12292
  154.8 162.2 %all-gather.5.cloned.1.call-start = ((), (), s32[]{:S(2)}) async-start(), calls=%async_computation.3 | async-start | bytes 17825792 | tf_op jit(solution)/shard_map/all_gather | solution.py:96
  317.1 36.3 %copy-start.2 = (bf16[256,1024]{1,0:T(8,128)(2,1)S(1)}, bf16[256,1024]{1,0:T(8,128)(2,1)}, u32[]{:S(2)}) copy-start(bf16[256,1024]{1,0:T(8,128)(2,1)} %param.23) | copy-start | bytes 1572868
  328.9 25.7 %copy-start.3 = (bf16[256,1024]{1,0:T(8,128)(2,1)}, bf16[256,1024]{1,0:T(8,128)(2,1)S(1)}, u32[]{:S(2)}) copy-start(bf16[256,1024]{1,0:T(8,128)(2,1)S(1)} %get-tuple-element.100) | copy-start | bytes 1572868
Sparse Core Ops, SparseCore 0:
  155.0 71.0 all-gather.2
  227.8 89.2 all-gather.4
where the time goes:
time: 362 us; the launch traced here: 361 us
  waiting for transfers between devices  173 us (48%)
  matrix products  80 us (22%)
  blocking collectives  43.5 us (12%)
  local copies, waits for them, and re-layouts  19.9 us (5%)
  other arithmetic  18.7 us (5%)
  between operations  15.4 us (4%)
  starting transfers between devices  5.93 us (2%)
  loops' own time  5.21 us (1%)
    all_gather x1, waiting for transfers between devices, local(): lax.all_gather(out_weight, 'seq', axis=0, tiled=True)  91 us
    all_gather x1, waiting for transfers between devices, local(): full_context = lax.all_gather(context, 'heads', axis=1, tiled=True)  69.8 us
    dot_general x8, matrix products, head_scores(): lax.dot_general(query_head, key_block, (((1,), (1,)), ((), ())), preferre...  44.9 us
    psum x1, blocking collectives, local(): lax.psum((jnp.sum(hidden * hidden, axis=1), jnp.sum(hidden * scaled, axis...  24.4 us
    dot_general x8, matrix products, one_head(): jnp.dot(probs.astype(jnp.bfloat16), values_here, preferred_element_type=j...  21.5 us
    all_to_all x1, blocking collectives, local(): lax.all_to_all(merged, 'seq', split_axis=0, concat_axis=0, tiled=True)  19.1 us
    reduce_sum x8, other arithmetic, one_head(): total = jnp.sum(probs, axis=1, keepdims=True)  16.8 us
    dot_general x1, matrix products, local(): jnp.dot(full_context, lax.all_gather(out_weight, 'seq', axis=0, tiled=Tru...  11.8 us
  transfers between devices with their start and end apart: 3, of which 3 were waited for; matrix products, arithmetic and copies ran while one was open for 1% of the time, Pallas kernels for 0%

commit v1 on v0

--- a/solution.py
+++ b/solution.py
@@ -90,7 +90,7 @@
         preferred_element_type=jnp.float32,
     )
     context = context.astype(jnp.bfloat16).reshape(tok_rows, q_width)
-    full_context = lax.all_gather(context, "heads", axis=1, tiled=True)
+    full_context = jnp.concatenate(lax.all_gather(context, "heads"), axis=1)
     branch = jnp.dot(
         full_context,
         lax.all_gather(out_weight, "seq", axis=0, tiled=True),

time: 362 us -> 362 us (level)
  waiting for transfers between devices: 173 us -> 166 us
  local copies, waits for them, and re-layouts: 19.9 us -> 26.3 us
    all_gather x1, waiting for transfers between devices: 91 us -> 84.6 us  [local(): lax.all_gather(out_weight, 'seq', axis=0, tiled=True)]
    all_gather x0 -> x1, local copies, waits for them, and re-layouts: none -> 6.45 us  [local(): full_context = jnp.concatenate(lax.all_gather(context, 'heads'), axis=1)]
  transfers between devices with their start and end apart: 3 -> 3, of which waited for: 3 -> 3; matrix products, arithmetic and copies ran while one was open for 1% -> 3% of each run, Pallas kernels for 0% -> 0%
where the time goes in v1:
time: 362 us; the launch traced here: 361 us
  waiting for transfers between devices  166 us (46%)
  matrix products  80 us (22%)
  blocking collectives  43.5 us (12%)
  local copies, waits for them, and re-layouts  26.3 us (7%)
  other arithmetic  18.7 us (5%)
  between operations  15.4 us (4%)
  starting transfers between devices  5.93 us (2%)
  loops' own time  5.21 us (1%)
    all_gather x1, waiting for transfers between devices, local(): lax.all_gather(out_weight, 'seq', axis=0, tiled=True)  84.6 us
    all_gather x1, waiting for transfers between devices, local(): full_context = jnp.concatenate(lax.all_gather(context, 'heads'), axis=1)  69.8 us
    dot_general x8, matrix products, head_scores(): lax.dot_general(query_head, key_block, (((1,), (1,)), ((), ())), preferre...  44.9 us
    psum x1, blocking collectives, local(): lax.psum((jnp.sum(hidden * hidden, axis=1), jnp.sum(hidden * scaled, axis...  24.4 us
    dot_general x8, matrix products, one_head(): jnp.dot(probs.astype(jnp.bfloat16), values_here, preferred_element_type=j...  21.5 us
    all_to_all x1, blocking collectives, local(): lax.all_to_all(merged, 'seq', split_axis=0, concat_axis=0, tiled=True)  19.1 us
    reduce_sum x8, other arithmetic, one_head(): total = jnp.sum(probs, axis=1, keepdims=True)  16.8 us
    dot_general x1, matrix products, local(): jnp.dot(full_context, lax.all_gather(out_weight, 'seq', axis=0, tiled=Tru...  11.9 us
  transfers between devices with their start and end apart: 3, of which 3 were waited for; matrix products, arithmetic and copies ran while one was open for 3% of the time, Pallas kernels for 0%

profile of v1, /device:TPU:0, one launch (start us, length us, event | category | flops | bytes accessed | tf_op | source)
XLA Modules:
  0.0 361.4 jit_solution(7398622198924341694)
XLA Ops:
  7.2 0.8 reshape.79
  9.3 2.0 copy.39
  11.2 5.7 %all-to-all-start = ((bf16[16,2,16,1024]{3,1,2,0:T(2,128)(2,1)}), bf16[16,2,16,1024]{3,1,2,0:T(2,128)(2,1)}, u32[]{:S(2)}, u32[]{:S(2)}) async-start(bf16[16,2,16,1024]{3,1,2,0:T(2,128)(2,1)} %copy.39), calls=%async_computation | async-start | bytes 2097152 | tf_op jit(solution)/shard_map/all_to_all | solution.py:68
  18.6 3.4 slice_bitcast_fusion
  21.9 11.6 %all-to-all-done = bf16[16,2,16,1024]{3,1,2,0:T(2,128)(2,1)} async-done(((bf16[16,2,16,1024]{3,1,2,0:T(2,128)(2,1)}), bf16[16,2,16,1024]{3,1,2,0:T(2,128)(2,1)}, u32[]{:S(2)}, u32[]{:S(2)}) %all-to-all-start) | async-done | bytes 1048608 | tf_op jit(solution)/shard_map/all_to_all | solution.py:68
  33.5 2.5 copy.40
  36.0 95.0 %while.11 = (s32[]{:T(128)}, bf16[8,512,128]{2,1,0:T(8,128)(2,1)}, s32[]{:T(128)}, s32[8]{0:T(128)S(1)}, bf16[512,1024]{1,0:T(8,128)(2,1)}, /*index=5*/bf16[6528...) while((s32[]{:T(128)}, bf16[8,512,128]{2,1,0:T(8,128)(2,1)}, ...), condition=%wide.region_6.7_spmd.clone, body=%wide.region_3.6_spmd.clone.sunk | while | flops 1741493632 | bytes 43744824 | solution.py:83
  36.0 0.6 dynamic_slice.29
  37.5 5.6 %fusion.52 = (f32[512]{0:T(512)S(1)}, f32[512,6528]{1,0:T(8,128)S(1)}) fusion(bf16[6528,128]{1,0:T(8,128)(2,1)} %get-tuple-element.183, bf16[512,1024]{1,0:T(8,128)(2,1)} %get-tuple-element.182, s32[]{:T(128)S(6)} %select_n.24, pred[6528]{0:T(1024)(128)(4,1)S(1)} %iota_compare_fusion.6, s32[512]{0:T(512)S(1)} %mul.129), kind=kOutput, calls=%fused_computation.51.clone.1 | convolution fusion | flops 872349184 | bytes 15182212 | tf_op jit(solution)/shard_map/while/body/eval_jaxpr/dot_general | solution.py:18
  43.1 2.1 fusion.53
  45.2 2.7 fusion.54
  47.9 0.6 dynamic_slice.29
  49.3 5.6 %fusion.52 = (f32[512]{0:T(512)S(1)}, f32[512,6528]{1,0:T(8,128)S(1)}) fusion(bf16[6528,128]{1,0:T(8,128)(2,1)} %get-tuple-element.183, bf16[512,1024]{1,0:T(8,128)(2,1)} %get-tuple-element.182, s32[]{:T(128)S(6)} %select_n.24, pred[6528]{0:T(1024)(128)(4,1)S(1)} %iota_compare_fusion.6, s32[512]{0:T(512)S(1)} %mul.129), kind=kOutput, calls=%fused_computation.51.clone.1 | convolution fusion | flops 872349184 | bytes 15182212 | tf_op jit(solution)/shard_map/while/body/eval_jaxpr/dot_general | solution.py:18
  54.9 2.1 fusion.53
  57.0 2.7 fusion.54
  59.7 0.6 dynamic_slice.29
  61.2 5.6 %fusion.52 = (f32[512]{0:T(512)S(1)}, f32[512,6528]{1,0:T(8,128)S(1)}) fusion(bf16[6528,128]{1,0:T(8,128)(2,1)} %get-tuple-element.183, bf16[512,1024]{1,0:T(8,128)(2,1)} %get-tuple-element.182, s32[]{:T(128)S(6)} %select_n.24, pred[6528]{0:T(1024)(128)(4,1)S(1)} %iota_compare_fusion.6, s32[512]{0:T(512)S(1)} %mul.129), kind=kOutput, calls=%fused_computation.51.clone.1 | convolution fusion | flops 872349184 | bytes 15182212 | tf_op jit(solution)/shard_map/while/body/eval_jaxpr/dot_general | solution.py:18
  66.8 2.1 fusion.53
  68.9 2.7 fusion.54
  71.6 0.6 dynamic_slice.29
  73.1 5.6 %fusion.52 = (f32[512]{0:T(512)S(1)}, f32[512,6528]{1,0:T(8,128)S(1)}) fusion(bf16[6528,128]{1,0:T(8,128)(2,1)} %get-tuple-element.183, bf16[512,1024]{1,0:T(8,128)(2,1)} %get-tuple-element.182, s32[]{:T(128)S(6)} %select_n.24, pred[6528]{0:T(1024)(128)(4,1)S(1)} %iota_compare_fusion.6, s32[512]{0:T(512)S(1)} %mul.129), kind=kOutput, calls=%fused_computation.51.clone.1 | convolution fusion | flops 872349184 | bytes 15182212 | tf_op jit(solution)/shard_map/while/body/eval_jaxpr/dot_general | solution.py:18
  78.7 2.1 fusion.53
  80.8 2.7 fusion.54
  83.5 0.6 dynamic_slice.29
  84.9 5.6 %fusion.52 = (f32[512]{0:T(512)S(1)}, f32[512,6528]{1,0:T(8,128)S(1)}) fusion(bf16[6528,128]{1,0:T(8,128)(2,1)} %get-tuple-element.183, bf16[512,1024]{1,0:T(8,128)(2,1)} %get-tuple-element.182, s32[]{:T(128)S(6)} %select_n.24, pred[6528]{0:T(1024)(128)(4,1)S(1)} %iota_compare_fusion.6, s32[512]{0:T(512)S(1)} %mul.129), kind=kOutput, calls=%fused_computation.51.clone.1 | convolution fusion | flops 872349184 | bytes 15182212 | tf_op jit(solution)/shard_map/while/body/eval_jaxpr/dot_general | solution.py:18
  90.6 2.1 fusion.53
  92.7 2.7 fusion.54
  95.3 0.6 dynamic_slice.29
  96.8 5.6 %fusion.52 = (f32[512]{0:T(512)S(1)}, f32[512,6528]{1,0:T(8,128)S(1)}) fusion(bf16[6528,128]{1,0:T(8,128)(2,1)} %get-tuple-element.183, bf16[512,1024]{1,0:T(8,128)(2,1)} %get-tuple-element.182, s32[]{:T(128)S(6)} %select_n.24, pred[6528]{0:T(1024)(128)(4,1)S(1)} %iota_compare_fusion.6, s32[512]{0:T(512)S(1)} %mul.129), kind=kOutput, calls=%fused_computation.51.clone.1 | convolution fusion | flops 872349184 | bytes 15182212 | tf_op jit(solution)/shard_map/while/body/eval_jaxpr/dot_general | solution.py:18
  102.4 2.1 fusion.53
  104.5 2.7 fusion.54
  107.2 0.6 dynamic_slice.29
  108.7 5.6 %fusion.52 = (f32[512]{0:T(512)S(1)}, f32[512,6528]{1,0:T(8,128)S(1)}) fusion(bf16[6528,128]{1,0:T(8,128)(2,1)} %get-tuple-element.183, bf16[512,1024]{1,0:T(8,128)(2,1)} %get-tuple-element.182, s32[]{:T(128)S(6)} %select_n.24, pred[6528]{0:T(1024)(128)(4,1)S(1)} %iota_compare_fusion.6, s32[512]{0:T(512)S(1)} %mul.129), kind=kOutput, calls=%fused_computation.51.clone.1 | convolution fusion | flops 872349184 | bytes 15182212 | tf_op jit(solution)/shard_map/while/body/eval_jaxpr/dot_general | solution.py:18
  114.3 2.1 fusion.53
  116.4 2.7 fusion.54
  120.6 5.6 %fusion.52 = (f32[512]{0:T(512)S(1)}, f32[512,6528]{1,0:T(8,128)S(1)}) fusion(bf16[6528,128]{1,0:T(8,128)(2,1)} %get-tuple-element.183, bf16[512,1024]{1,0:T(8,128)(2,1)} %get-tuple-element.182, s32[]{:T(128)S(6)} %select_n.24, pred[6528]{0:T(1024)(128)(4,1)S(1)} %iota_compare_fusion.6, s32[512]{0:T(512)S(1)} %mul.129), kind=kOutput, calls=%fused_computation.51.clone.1 | convolution fusion | flops 872349184 | bytes 15182212 | tf_op jit(solution)/shard_map/while/body/eval_jaxpr/dot_general | solution.py:18
  126.2 2.1 fusion.53
  128.3 2.7 fusion.54
  131.0 1.9 copy.42
  133.4 19.1 %all_to_all.10 = bf16[16,2,16,1024]{3,2,1,0:T(8,128)(2,1)S(1)} all-to-all(bf16[16,2,16,1024]{3,2,1,0:T(8,128)(2,1)S(1)} %reshape.83), channel_id=1, replica_groups=mesh['seq'=16,'heads'=8] {'seq'}, dimensions={0} | all-to-all | bytes 2097152 | tf_op jit(solution)/shard_map/all_to_all | solution.py:85
  152.5 1.2 convolution_convert_fusion.1
  153.7 1.1 copy.44
  156.2 69.8 %all-gather.3.cloned.1.call-done = bf16[8,256,1024]{2,1,0:T(8,128)(2,1)} async-done(((bf16[1,256,1024]{2,1,0:T(8,128)(2,1)}), bf16[8,256,1024]{2,1,0:T(8,128)(2,1)}) %all-gather.3.cloned.1.call-update) | async-done | bytes 4194320 | tf_op jit(solution)/shard_map/all_gather | solution.py:93
  226.0 6.5 %copy.45 = bf16[8,256,1024]{1,2,0:T(8,128)(2,1)} copy(bf16[8,256,1024]{2,1,0:T(8,128)(2,1)} %all-gather.3.cloned.1.call-done) | data formatting | bytes 8388608 | tf_op jit(solution)/shard_map/all_gather | solution.py:93
  232.4 84.6 %all-gather.5.cloned.1.call-done = bf16[8192,1024]{1,0:T(8,128)(2,1)} async-done(((bf16[512,1024]{1,0:T(8,128)(2,1)}), bf16[8192,1024]{1,0:T(8,128)(2,1)}) %all-gather.5.cloned.1.call-update) | async-done | bytes 16777232 | tf_op jit(solution)/shard_map/all_gather | solution.py:96
  317.0 11.9 %fusion.24 = (f32[256]{0:T(256)S(1)}, f32[256]{0:T(256)S(1)}, bf16[256,1024]{1,0:T(8,128)(2,1)S(1)}) fusion(bf16[256,1024]{1,0:T(8,128)(2,1)S(1)} %copy-done.1, f32[1024]{0:T(1024)S(1)} %copy-done.5, bf16[256,8192]{0,1:T(8,128)(2,1)} %bitcast.42, bf16[8192,1024]{1,0:T(8,128)(2,1)} %all-gather.5.cloned.1.call-done, f32[]{:T(128)} %bitcast, ...), kind=kOutput, calls=%fused_computation.26 | convolution fusion | flops 4297850880 | bytes 22550532 | tf_op jit(solution)/shard_map/dot_general | solution.py:94
  328.9 24.4 %all-reduce = (f32[256]{0:T(256)S(1)}, f32[256]{0:T(256)S(1)}) all-reduce(f32[256]{0:T(256)S(1)} %get-tuple-element.73, f32[256]{0:T(256)S(1)} %get-tuple-element.72), channel_id=1, replica_groups=mesh['seq'=16,'heads'=8] {'heads'}, use_global_device_ids=true, to_apply=%region_10.11 | all-reduce | flops 512 | bytes 4096 | tf_op jit(solution)/shard_map/psum | solution.py:102
  353.3 1.3 fusion.26
  (62 shorter events, 5.7 us)
Async XLA Ops:
  7.2 1.1 copy-start
  7.2 10.0 %copy-start.6 = (s32[256]{0:T(256)S(1)}, s32[256]{0:T(256)}, u32[]{:S(2)}) copy-start(s32[256]{0:T(256)} %param.20) | copy-start | bytes 3076
  7.2 10.3 %copy-start.7 = (s32[16]{0:T(128)S(1)}, s32[16]{0:T(128)}, u32[]{:S(2)}) copy-start(s32[16]{0:T(128)} %param.18) | copy-start | bytes 196
  11.2 22.3 %all-to-all-start = ((bf16[16,2,16,1024]{3,1,2,0:T(2,128)(2,1)}), bf16[16,2,16,1024]{3,1,2,0:T(2,128)(2,1)}, u32[]{:S(2)}, u32[]{:S(2)}) async-start(bf16[16,2,16,1024]{3,1,2,0:T(2,128)(2,1)} %copy.39), calls=%async_computation | async-start | bytes 2097152 | tf_op jit(solution)/shard_map/all_to_all | solution.py:68
  16.9 209.1 %all-gather.3.cloned.1.call-start = ((), (), s32[]{:S(2)}) async-start(), calls=%async_computation.2 | async-start | bytes 4718592 | tf_op jit(solution)/shard_map/all_gather | solution.py:93
  152.4 164.6 %copy-start.1 = (bf16[256,1024]{1,0:T(8,128)(2,1)S(1)}, bf16[256,1024]{1,0:T(8,128)(2,1)}, u32[]{:S(2)}) copy-start(bf16[256,1024]{1,0:T(8,128)(2,1)} %param.22) | copy-start | bytes 1572868
  152.4 164.6 %copy-start.3 = (bf16[256,1024]{1,0:T(8,128)(2,1)S(1)}, bf16[256,1024]{1,0:T(8,128)(2,1)}, u32[]{:S(2)}) copy-start(bf16[256,1024]{1,0:T(8,128)(2,1)} %param.13) | copy-start | bytes 1572868
  152.5 164.6 %copy-start.5 = (f32[1024]{0:T(1024)S(1)}, f32[1024]{0:T(1024)}, u32[]{:S(2)}) copy-start(f32[1024]{0:T(1024)} %param.21) | copy-start | bytes 12292
  154.8 162.2 %all-gather.5.cloned.1.call-start = ((), (), s32[]{:S(2)}) async-start(), calls=%async_computation.3 | async-start | bytes 17825792 | tf_op jit(solution)/shard_map/all_gather | solution.py:96
  317.0 36.3 %copy-start.4 = (bf16[256,1024]{1,0:T(8,128)(2,1)S(1)}, bf16[256,1024]{1,0:T(8,128)(2,1)}, u32[]{:S(2)}) copy-start(bf16[256,1024]{1,0:T(8,128)(2,1)} %param.23) | copy-start | bytes 1572868
  328.9 25.7 %copy-start.2 = (bf16[256,1024]{1,0:T(8,128)(2,1)}, bf16[256,1024]{1,0:T(8,128)(2,1)S(1)}, u32[]{:S(2)}) copy-start(bf16[256,1024]{1,0:T(8,128)(2,1)S(1)} %get-tuple-element.100) | copy-start | bytes 1572868
Sparse Core Ops, SparseCore 0:
  154.9 71.0 all-gather.2
  227.7 89.2 all-gather.4
